TPU v7x, 32 devices: a whole 2x2x4 slice. The times are simulated.
32 devices in a mesh: dp: 4 (over x, core), fsdp: 8 (over z, y).
Axes of the slice: x: 2, y: 2, z: 4, core: 2. Of those that a mesh axis runs over, the one named last changes fastest.
Arguments:
- inputs: bfloat16 [64, 256, 768], P(('dp', 'fsdp')), may hold values from -6 to 6
- cotangent: bfloat16 [64, 256, 768], P(('dp', 'fsdp')), may hold values from -6 to 6
- image_shape: int32 [64, 2], P(('dp', 'fsdp')), may hold values from 8 to 16, as said below
- time_bins: int32 [64], P(('dp', 'fsdp')), may hold values from 0 to 999
- time_table: float32 [1000, 768], replicated, may hold values from -6 to 6
- modulation_master: float32 [6, 768, 768], P(None, 'fsdp'), may hold values from -0.21875 to 0.21875
- projection_master: float32 [3, 768, 768], P(None, 'fsdp'), may hold values from -0.21875 to 0.21875
- output_master: float32 [768, 768], P('fsdp'), may hold values from -1.75 to 1.75
- expand_master: float32 [2, 768, 2048], P(None, 'fsdp'), may hold values from -0.21875 to 0.21875
- shrink_master: float32 [2048, 768], P(None, 'fsdp'), may hold values from -0.125 to 0.125
- modulation_moment: float32 [6, 768, 768], P(None, 'fsdp'), may hold values from -80 to 80
- projection_moment: float32 [3, 768, 768], P(None, 'fsdp'), may hold values from -448 to 448
- output_moment: float32 [768, 768], P('fsdp'), may hold values from -80 to 80
- expand_moment: float32 [2, 768, 2048], P(None, 'fsdp'), may hold values from -80 to 80
- shrink_moment: float32 [2048, 768], P(None, 'fsdp'), may hold values from -80 to 80
Outputs:
- block_output: bfloat16 [64, 256, 768], P(('dp', 'fsdp'))
- input_gradient: float32 [64, 256, 768], P(('dp', 'fsdp'))
- modulation_gradient: float32 [6, 768, 768], P(None, 'fsdp')
- projection_gradient: float32 [3, 768, 768], P(None, 'fsdp')
- output_gradient: float32 [768, 768], P('fsdp')
- expand_gradient: float32 [2, 768, 2048], P(None, 'fsdp')
- shrink_gradient: float32 [2048, 768], P(None, 'fsdp')
- modulation_weight: float32 [6, 768, 768], P(None, 'fsdp')
- projection_weight: float32 [3, 768, 768], P(None, 'fsdp')
- output_weight: float32 [768, 768], P('fsdp')
- expand_weight: float32 [2, 768, 2048], P(None, 'fsdp')
- shrink_weight: float32 [2048, 768], P(None, 'fsdp')
- modulation_state: float32 [6, 768, 768], P(None, 'fsdp')
- projection_state: float32 [3, 768, 768], P(None, 'fsdp')
- output_state: float32 [768, 768], P('fsdp')
- expand_state: float32 [2, 768, 2048], P(None, 'fsdp')
- shrink_state: float32 [2048, 768], P(None, 'fsdp')
Inputs may be any that keep to these rules, and one draw needn't show every extreme that they name: Image b has image_shape[b, 0] patch rows and image_shape[b, 1] patch columns; in every draw some image is 16 x 16, filling all 256 slots.
All inputs are finite; a program needn't handle non-finite values.
Results may differ from a plain program's by a relative error of at most 0.02.
The roundings to bfloat16 on the way count: a program that leaves them out, or rounds other values in their place, can miss the bound.
Values may be sent and summed in bfloat16 or wider, within the bound.
No kernel may reach another device: no remote copies, remote signals or barrier semaphores. Data moves between devices by JAX's collectives and lax.ppermute only.
A program may use at most 192 MiB of HBM per device.

v0:
```python
import jax
import jax.numpy as jnp
from jax import lax
from jax.sharding import PartitionSpec as P

D = 768
HEADS = 12
HDIM = 64
FF = 2048
NS_ITERS = 5
NORM_EPS = 1e-06
FROBENIUS_EPS = 1e-07
COEFF_FIRST = 3.4445
COEFF_SECOND = -4.775
COEFF_THIRD = 2.0315
MOMENTUM_DECAY = 0.9
LEARN_RATE = 1.0
HIGHEST = lax.Precision.HIGHEST


def swish_value(values):
    return values / (1.0 + jnp.exp(-values))


def layer_norm(values):
    centred = values - jnp.mean(values, axis=-1, keepdims=True)
    inverse = lax.rsqrt(jnp.mean(centred * centred, axis=-1, keepdims=True) + NORM_EPS)
    return (centred * inverse, inverse)


def norm_back(incoming, normed, inverse):
    return inverse * (
        incoming
        - jnp.mean(incoming, axis=-1, keepdims=True)
        - normed * jnp.mean(incoming * normed, axis=-1, keepdims=True)
    )


def rotate(tensor):
    first, second, third, fourth = jnp.split(tensor, 4, axis=-1)
    return jnp.concatenate([-second, first, -fourth, third], axis=-1)


def rope_tables(extents, positions):
    quarter = HDIM // 4
    places = jnp.arange(positions, dtype=jnp.int32)
    widths = extents[:, 1]
    row_place = (places[None, :] // widths[:, None]).astype(jnp.float32)
    col_place = (places[None, :] % widths[:, None]).astype(jnp.float32)
    frequency = 10000.0 ** (-jnp.arange(quarter).astype(jnp.float32) / quarter)
    row_angle = row_place[:, :, None] * frequency
    col_angle = col_place[:, :, None] * frequency
    cosine_table = jnp.concatenate(
        [jnp.cos(row_angle), jnp.cos(row_angle), jnp.cos(col_angle), jnp.cos(col_angle)], axis=-1
    )
    sine_table = jnp.concatenate(
        [jnp.sin(row_angle), jnp.sin(row_angle), jnp.sin(col_angle), jnp.sin(col_angle)], axis=-1
    )
    return (cosine_table[:, :, None, :], sine_table[:, :, None, :])


def forward(weights, stream, activated, key_mask, cosine_table, sine_table):
    modulation_weight, projection_weight, output_weight, expand_weight, shrink_weight = weights
    images_here, positions, features = stream.shape
    modulation = jnp.einsum(
        "bd,kde->kbe", activated, modulation_weight, preferred_element_type=jnp.float32
    )
    shift_one, scale_one, gate_one, shift_two, scale_two, gate_two = [
        modulation[which][:, None, :] for which in range(6)
    ]
    normed_one, inverse_one = layer_norm(stream)
    first_input = (normed_one * (1.0 + scale_one) + shift_one).astype(jnp.bfloat16)
    projected = jnp.einsum(
        "bsd,kde->kbse", first_input, projection_weight, preferred_element_type=jnp.float32
    )
    projected = projected.reshape(3, images_here, positions, HEADS, HDIM)
    query_rot = (projected[0] * cosine_table + rotate(projected[0]) * sine_table).astype(
        jnp.bfloat16
    )
    key_rot = (projected[1] * cosine_table + rotate(projected[1]) * sine_table).astype(jnp.bfloat16)
    value_heads = projected[2].astype(jnp.bfloat16)
    scores = jnp.einsum(
        "bqhd,bkhd->bhqk", query_rot, key_rot, preferred_element_type=jnp.float32
    ) * HDIM ** (-0.5)
    scores = jnp.where(key_mask[:, None, None, :], scores, -1000000000.0)
    exponent = jnp.exp(scores - jnp.max(scores, axis=-1, keepdims=True))
    softmax_out = exponent / jnp.sum(exponent, axis=-1, keepdims=True)
    softmax_low = softmax_out.astype(jnp.bfloat16)
    attended = jnp.einsum(
        "bhqk,bkhd->bqhd", softmax_low, value_heads, preferred_element_type=jnp.float32
    )
    attended = attended.astype(jnp.bfloat16).reshape(images_here, positions, features)
    attention = jnp.einsum(
        "bsd,de->bse", attended, output_weight, preferred_element_type=jnp.float32
    )
    middle = stream + gate_one * attention
    normed_two, inverse_two = layer_norm(middle)
    second_input = (normed_two * (1.0 + scale_two) + shift_two).astype(jnp.bfloat16)
    expanded = jnp.einsum(
        "bsd,kdf->kbsf", second_input, expand_weight, preferred_element_type=jnp.float32
    )
    gate_pre = expanded[0]
    up_pre = expanded[1]
    hidden = (swish_value(gate_pre) * up_pre).astype(jnp.bfloat16)
    branch_out = jnp.einsum(
        "bsf,fd->bsd", hidden, shrink_weight, preferred_element_type=jnp.float32
    )
    result = middle + gate_two * branch_out
    saved = (
        modulation,
        normed_one,
        inverse_one,
        first_input,
        query_rot,
        key_rot,
        value_heads,
        softmax_out,
        softmax_low,
        attended,
        attention,
        normed_two,
        inverse_two,
        second_input,
        gate_pre,
        up_pre,
        hidden,
        branch_out,
    )
    return (result, saved)


def backward(weights, activated, saved, upstream, cosine_table, sine_table):
    modulation_weight, projection_weight, output_weight, expand_weight, shrink_weight = weights
    (
        modulation,
        normed_one,
        inverse_one,
        first_input,
        query_rot,
        key_rot,
        value_heads,
        softmax_out,
        softmax_low,
        attended,
        attention,
        normed_two,
        inverse_two,
        second_input,
        gate_pre,
        up_pre,
        hidden,
        branch_out,
    ) = saved
    images_here, positions, features = upstream.shape
    shift_one, scale_one, gate_one, shift_two, scale_two, gate_two = [
        modulation[which][:, None, :] for which in range(6)
    ]
    grad_gate_two = jnp.sum(upstream * branch_out, axis=1)
    grad_branch = (gate_two * upstream).astype(jnp.bfloat16)
    grad_shrink = jnp.einsum("bsf,bsd->fd", hidden, grad_branch, preferred_element_type=jnp.float32)
    grad_hidden = jnp.einsum(
        "bsd,fd->bsf", grad_branch, shrink_weight, preferred_element_type=jnp.float32
    )
    sigmoid_gate = 1.0 / (1.0 + jnp.exp(-gate_pre))
    grad_gate = grad_hidden * up_pre * sigmoid_gate * (1.0 + gate_pre * (1.0 - sigmoid_gate))
    grad_up = grad_hidden * gate_pre * sigmoid_gate
    grad_expand_in = jnp.stack([grad_gate, grad_up]).astype(jnp.bfloat16)
    grad_expand = jnp.einsum(
        "bsd,kbsf->kdf", second_input, grad_expand_in, preferred_element_type=jnp.float32
    )
    grad_second = jnp.einsum(
        "kbsf,kdf->bsd", grad_expand_in, expand_weight, preferred_element_type=jnp.float32
    )
    grad_scale_two = jnp.sum(grad_second * normed_two, axis=1)
    grad_shift_two = jnp.sum(grad_second, axis=1)
    grad_stream = upstream + norm_back(grad_second * (1.0 + scale_two), normed_two, inverse_two)
    grad_gate_one = jnp.sum(grad_stream * attention, axis=1)
    grad_attention = (gate_one * grad_stream).astype(jnp.bfloat16)
    grad_output = jnp.einsum(
        "bsd,bse->de", attended, grad_attention, preferred_element_type=jnp.float32
    )
    grad_attended = jnp.einsum(
        "bse,de->bsd", grad_attention, output_weight, preferred_element_type=jnp.float32
    )
    grad_attended = grad_attended.astype(jnp.bfloat16).reshape(images_here, positions, HEADS, HDIM)
    grad_soft = jnp.einsum(
        "bqhd,bkhd->bhqk", grad_attended, value_heads, preferred_element_type=jnp.float32
    )
    grad_values = jnp.einsum(
        "bhqk,bqhd->bkhd", softmax_low, grad_attended, preferred_element_type=jnp.float32
    )
    grad_scores = softmax_out * (
        grad_soft - jnp.sum(grad_soft * softmax_out, axis=-1, keepdims=True)
    )
    grad_scores = grad_scores.astype(jnp.bfloat16)
    grad_qrot = jnp.einsum(
        "bhqk,bkhd->bqhd", grad_scores, key_rot, preferred_element_type=jnp.float32
    ) * HDIM ** (-0.5)
    grad_krot = jnp.einsum(
        "bhqk,bqhd->bkhd", grad_scores, query_rot, preferred_element_type=jnp.float32
    ) * HDIM ** (-0.5)
    grad_query = grad_qrot * cosine_table - rotate(grad_qrot * sine_table)
    grad_key = grad_krot * cosine_table - rotate(grad_krot * sine_table)
    grad_project_in = (
        jnp.stack([grad_query, grad_key, grad_values])
        .reshape(3, images_here, positions, features)
        .astype(jnp.bfloat16)
    )
    grad_projection = jnp.einsum(
        "bsd,kbse->kde", first_input, grad_project_in, preferred_element_type=jnp.float32
    )
    grad_first = jnp.einsum(
        "kbse,kde->bsd", grad_project_in, projection_weight, preferred_element_type=jnp.float32
    )
    grad_scale_one = jnp.sum(grad_first * normed_one, axis=1)
    grad_shift_one = jnp.sum(grad_first, axis=1)
    grad_stream = grad_stream + norm_back(grad_first * (1.0 + scale_one), normed_one, inverse_one)
    grad_modulation_in = jnp.stack(
        [
            grad_shift_one,
            grad_scale_one,
            grad_gate_one,
            grad_shift_two,
            grad_scale_two,
            grad_gate_two,
        ]
    ).astype(jnp.bfloat16)
    grad_modulation = jnp.einsum(
        "bd,kbe->kde", activated, grad_modulation_in, preferred_element_type=jnp.float32
    )
    return (grad_stream, (grad_modulation, grad_projection, grad_output, grad_expand, grad_shrink))


def orthogonalize(matrices):
    norms_sq = jnp.sum(matrices * matrices, axis=(1, 2), keepdims=True)
    current = matrices / (jnp.sqrt(norms_sq) + FROBENIUS_EPS)
    for iteration in range(NS_ITERS):
        gram = jnp.einsum("nik,njk->nij", current, current, precision=HIGHEST)
        poly = COEFF_SECOND * gram + COEFF_THIRD * jnp.einsum(
            "nij,njk->nik", gram, gram, precision=HIGHEST
        )
        current = COEFF_FIRST * current + jnp.einsum(
            "nij,njk->nik", poly, current, precision=HIGHEST
        )
    return current


def local(
    inputs,
    cotangent,
    image_shape,
    time_bins,
    time_table,
    modulation_master,
    projection_master,
    output_master,
    expand_master,
    shrink_master,
    modulation_moment,
    projection_moment,
    output_moment,
    expand_moment,
    shrink_moment,
):
    masters = (modulation_master, projection_master, output_master, expand_master, shrink_master)
    moments = (modulation_moment, projection_moment, output_moment, expand_moment, shrink_moment)
    gathered = (
        lax.all_gather(modulation_master.astype(jnp.bfloat16), "fsdp", axis=1, tiled=True),
        lax.all_gather(projection_master.astype(jnp.bfloat16), "fsdp", axis=1, tiled=True),
        lax.all_gather(output_master.astype(jnp.bfloat16), "fsdp", axis=0, tiled=True),
        lax.all_gather(expand_master.astype(jnp.bfloat16), "fsdp", axis=1, tiled=True),
        lax.all_gather(shrink_master.astype(jnp.bfloat16), "fsdp", axis=1, tiled=True),
    )
    stream = inputs.astype(jnp.float32)
    positions = stream.shape[1]
    places = jnp.arange(positions, dtype=jnp.int32)
    lengths = image_shape[:, 0] * image_shape[:, 1]
    key_mask = places[None, :] < lengths[:, None]
    cosine_table, sine_table = rope_tables(image_shape, positions)
    selector = (
        time_bins[:, None] == jnp.arange(time_table.shape[0], dtype=jnp.int32)[None, :]
    ).astype(jnp.float32)
    condition = jnp.dot(selector, time_table, precision=HIGHEST)
    activated = swish_value(condition).astype(jnp.bfloat16)
    result, saved = forward(gathered, stream, activated, key_mask, cosine_table, sine_table)
    backing = (
        lax.all_gather(modulation_master.astype(jnp.bfloat16), "fsdp", axis=1, tiled=True),
        lax.all_gather(projection_master.astype(jnp.bfloat16), "fsdp", axis=1, tiled=True),
        lax.all_gather(output_master.astype(jnp.bfloat16), "fsdp", axis=0, tiled=True),
        lax.all_gather(expand_master.astype(jnp.bfloat16), "fsdp", axis=1, tiled=True),
        lax.all_gather(shrink_master.astype(jnp.bfloat16), "fsdp", axis=1, tiled=True),
    )
    saved = forward(backing, stream, activated, key_mask, cosine_table, sine_table)[1]
    upstream = cotangent.astype(jnp.float32) * key_mask[:, :, None].astype(jnp.float32)
    input_gradient, partials = backward(
        backing, activated, saved, upstream, cosine_table, sine_table
    )
    devices = lax.axis_size("fsdp")
    rows_local = modulation_master.shape[1]
    shards = (
        lax.psum_scatter(partials[0], "fsdp", scatter_dimension=1, tiled=True),
        lax.psum_scatter(partials[1], "fsdp", scatter_dimension=1, tiled=True),
        lax.psum_scatter(partials[2], "fsdp", scatter_dimension=0, tiled=True),
        lax.psum_scatter(partials[3], "fsdp", scatter_dimension=1, tiled=True),
        lax.psum_scatter(partials[4], "fsdp", scatter_dimension=1, tiled=True),
    )
    totals = lax.psum((shards[0], shards[1], shards[2], shards[3], shards[4]), "dp")
    states = tuple((MOMENTUM_DECAY * moment + total for moment, total in zip(moments, totals)))
    feeds = tuple((total + MOMENTUM_DECAY * state for total, state in zip(totals, states)))
    pieces = (
        [feeds[0][which] for which in range(6)]
        + [feeds[1][which] for which in range(3)]
        + [feeds[2], feeds[3][0], feeds[3][1], feeds[4].T]
    )
    slot_count = (len(pieces) + devices - 1) // devices
    padded = [jnp.pad(piece, ((0, 0), (0, FF - piece.shape[1]))) for piece in pieces]
    padded = padded + [jnp.zeros((rows_local, FF), jnp.float32)] * (
        slot_count * devices - len(pieces)
    )
    outgoing = jnp.stack(padded).reshape(slot_count, devices, rows_local, FF)
    received = lax.all_to_all(outgoing, "fsdp", split_axis=1, concat_axis=1, tiled=True)
    items_here = received.shape[0]
    whole = orthogonalize(received.reshape(items_here, devices * rows_local, FF))
    returned = lax.all_to_all(
        whole.reshape(items_here, devices, rows_local, FF).astype(jnp.bfloat16),
        "fsdp",
        split_axis=1,
        concat_axis=1,
        tiled=True,
    ).astype(jnp.float32)
    returned = returned.reshape(slot_count * devices, rows_local, FF)
    modulation_step = returned[0:6, :, :D]
    projection_step = returned[6:9, :, :D]
    output_step = returned[9, :, :D]
    expand_step = returned[10:12] * (FF / D) ** 0.5
    shrink_step = returned[12].T
    steps_all = (modulation_step, projection_step, output_step, expand_step, shrink_step)
    updated = tuple((master - LEARN_RATE * step for master, step in zip(masters, steps_all)))
    return (
        result.astype(jnp.bfloat16),
        input_gradient,
        totals[0],
        totals[1],
        totals[2],
        totals[3],
        totals[4],
        updated[0],
        updated[1],
        updated[2],
        updated[3],
        updated[4],
        states[0],
        states[1],
        states[2],
        states[3],
        states[4],
    )


def solution(mesh):
    placed = (
        P(("dp", "fsdp"), None, None),
        P(("dp", "fsdp"), None, None),
        P(("dp", "fsdp"), None),
        P(("dp", "fsdp")),
        P(),
        P(None, "fsdp", None),
        P(None, "fsdp", None),
        P("fsdp", None),
        P(None, "fsdp", None),
        P(None, "fsdp"),
        P(None, "fsdp", None),
        P(None, "fsdp", None),
        P("fsdp", None),
        P(None, "fsdp", None),
        P(None, "fsdp"),
    )
    return jax.shard_map(
        local,
        mesh=mesh,
        in_specs=placed,
        out_specs=(
            P(("dp", "fsdp"), None, None),
            P(("dp", "fsdp"), None, None),
            P(None, "fsdp", None),
            P(None, "fsdp", None),
            P("fsdp", None),
            P(None, "fsdp", None),
            P(None, "fsdp"),
            P(None, "fsdp", None),
            P(None, "fsdp", None),
            P("fsdp", None),
            P(None, "fsdp", None),
            P(None, "fsdp"),
            P(None, "fsdp", None),
            P(None, "fsdp", None),
            P("fsdp", None),
            P(None, "fsdp", None),
            P(None, "fsdp"),
        ),
        check_vma=False,
    )
```

profile of v0, /device:TPU:0, one launch (start us, length us, event | category | flops | bytes accessed | tf_op | source)
XLA Modules:
  0.0 2515.5 jit_solution(1578928121377472265)
XLA Ops:
  22.5 99.9 %all-gather.6.cloned.1.call-done = bf16[6,768,768]{2,1,0:T(8,128)(2,1)} async-done(((bf16[6,96,768]{2,1,0:T(8,128)(2,1)}), bf16[6,768,768]{2,1,0:T(8,128)(2,1)}) %all-gather.6.cloned.1.call-update) | async-done | bytes 7077904 | tf_op jit(solution)/shard_map/all_gather | solution.py:268
  126.4 62.1 %all-gather.8.cloned.1.call-done = bf16[3,768,768]{2,1,0:T(8,128)(2,1)} async-done(((bf16[3,96,768]{2,1,0:T(8,128)(2,1)}), bf16[3,768,768]{2,1,0:T(8,128)(2,1)}) %all-gather.8.cloned.1.call-update) | async-done | bytes 3538960 | tf_op jit(solution)/shard_map/all_gather | solution.py:269
  206.6 6.4 fusion.151
  217.5 13.3 all-gather.10.cloned.1.call-done
  234.7 96.6 %all-gather.12.cloned.1.call-done = bf16[2,768,2048]{2,1,0:T(8,128)(2,1)} async-done(((bf16[2,96,2048]{2,1,0:T(8,128)(2,1)}), bf16[2,768,2048]{2,1,0:T(8,128)(2,1)}) %all-gather.12.cloned.1.call-update) | async-done | bytes 6291472 | tf_op jit(solution)/shard_map/all_gather | solution.py:271
  331.3 8.9 fusion.34
  340.2 52.4 %all-gather.14.cloned.1.call-done = bf16[2048,768]{0,1:T(8,128)(2,1)} async-done(((bf16[2048,96]{0,1:T(8,128)(2,1)}), bf16[2048,768]{0,1:T(8,128)(2,1)}) %all-gather.14.cloned.1.call-update) | async-done | bytes 3145744 | tf_op jit(solution)/shard_map/all_gather | solution.py:272
  392.6 9.2 fusion.63
  403.7 6.8 convolution_bitcast_fusion.1
  410.5 19.4 copy.162
  430.0 8.1 fusion.85
  471.1 6.2 convolution_bitcast_fusion.3
  477.3 10.7 copy.206
  488.0 8.3 copy.212
  496.5 6.2 fusion.76
  502.8 7.0 convolution_bitcast_fusion
  509.8 17.6 copy.204
  527.3 16.0 copy.211
  547.3 6.3 convolution_bitcast_fusion.2
  555.5 270.9 %all-reduce.15.cloned.1.call-done = f32[2,768,2048]{2,0,1:T(2,128)} async-done(((f32[2,768,2048]{2,0,1:T(2,128)}), f32[2,768,2048]{2,0,1:T(2,128)}) %all-reduce.15.cloned.1.call-update) | async-done | bytes 12582928
  829.0 129.6 %reduce-scatter.15.cloned.1.call-done = f32[96,2304]{1,0:T(8,128)} async-done(((f32[768,2304]{1,0:T(8,128)}), f32[96,2304]{1,0:T(8,128)}) %reduce-scatter.15.cloned.1.call-update) | async-done | bytes 884752
  961.9 228.7 %reduce-scatter.13.cloned.1.call-done = f32[96,4608]{1,0:T(8,128)} async-done(((f32[768,4608]{1,0:T(8,128)}), f32[96,4608]{1,0:T(8,128)}) %reduce-scatter.13.cloned.1.call-update) | async-done | bytes 1769488
  1194.4 67.8 %reduce-scatter.11.cloned.1.call-done = f32[96,768]{1,0:T(8,128)} async-done(((f32[768,768]{1,0:T(8,128)}), f32[96,768]{1,0:T(8,128)}) %reduce-scatter.11.cloned.1.call-update) | async-done | bytes 294928 | tf_op jit(solution)/shard_map/reduce_scatter | solution.py:303
  1262.2 120.4 %reduce-scatter.17.cloned.1.call-done = f32[96,2048]{1,0:T(8,128)} async-done(((f32[768,2048]{1,0:T(8,128)}), f32[96,2048]{1,0:T(8,128)}) %reduce-scatter.17.cloned.1.call-update) | async-done | bytes 786448
  1387.1 116.7 %all-reduce.17.cloned.1.call-done = (f32[6,96,768]{1,2,0:T(8,128)}, f32[3,96,768]{1,2,0:T(8,128)}, f32[96,768]{1,0:T(8,128)}, f32[2,96,2048]{2,0,1:T(2,128)}, f32[2048,96]{0,1:T(8,128)}) async-done(((f32[6,96,768]{1,2,0:T(8,128)}, f32[3,96,768]{1,2,0:T(8,128)}, f32[96,768]{1,0:T(8,128)}, f32[2,96,2048]{2,0,1:T(2,128)}, f32[2048,96]{0,1:T(8,128)}), (f32[6,96,768]{1,2,0:T(8,128)}, f32[3,96,768]{1,2,0:T(8,128)}, ...) | async-done | bytes 5308432 | tf_op jit(solution)/shard_map/psum | solution.py:307
  1543.3 34.5 %stack.120 = f32[16,96,2048]{2,0,1:T(8,128)} concatenate(f32[1,96,2048]{2,0,1:T(1,128)} %copy.169, f32[1,96,2048]{2,0,1:T(1,128)} %copy.170, f32[1,96,2048]{2,0,1:T(1,128)} %copy.171, f32[1,96,2048]{2,0,1:T(1,128)} %copy.172, f32[1,96,2048]{2,0,1:T(1,128)} %copy.173, f32[1,96,2048]{2,0,1:T(1,128)} %copy.174, f32[1,96,2048]{2,0,1:T(1,128)} %copy.175, f32[1,96,2048]{2,0,1:T(1,128)} %copy.176, ...), dimensions={0} | concatenate | bytes 25165824 | tf_op jit(solution)/shard_map/stack | solution.py:320
  1577.8 16.4 copy.179
  1594.2 278.8 %all_to_all.10 = f32[2,8,96,2048]{3,2,0,1:T(8,128)S(1)} all-to-all(f32[2,8,96,2048]{3,2,0,1:T(8,128)} %copy.179), channel_id=1, replica_groups=mesh['dp'=4,'fsdp'=8] {'fsdp'}, dimensions={1} | all-to-all | bytes 25165824 | tf_op jit(solution)/shard_map/all_to_all | solution.py:321
  1877.5 11.3 copy.180
  1888.8 11.9 bitcast_divide_fusion
  1900.7 34.6 %fusion.155 = f32[2,768,768]{2,1,0:T(8,128)S(1)} fusion(f32[2,768,2048]{2,1,0:T(8,128)} %bitcast_divide_fusion), kind=kOutput, calls=%fused_computation.269 | convolution fusion | flops 28991029248 | bytes 17301504 | tf_op jit(solution)/shard_map/nik,njk->nij/dot_general | solution.py:238
  1935.3 13.3 fusion.156
  1948.6 35.0 %multiply_add_fusion.3 = f32[2,768,2048]{2,1,0:T(8,128)S(1)} fusion(f32[2,768,2048]{2,1,0:T(8,128)} %bitcast_divide_fusion, f32[2,768,768]{2,1,0:T(8,128)} %fusion.156, f32[2,768,768]{2,1,0:T(8,128)S(1)} %fusion.155), kind=kOutput, calls=%fused_computation.6 | convolution fusion | flops 29000859648 | bytes 34603008 | tf_op jit(solution)/shard_map/nij,njk->nik/dot_general | solution.py:242
  1983.7 31.3 %fusion.157 = f32[2,768,768]{2,1,0:T(8,128)S(1)} fusion(f32[2,768,2048]{2,1,0:T(8,128)S(1)} %multiply_add_fusion.3), kind=kOutput, calls=%fused_computation.271 | convolution fusion | flops 28991029248 | bytes 17301504 | tf_op jit(solution)/shard_map/nik,njk->nij/dot_general | solution.py:238
  2015.0 12.0 fusion.158
  2027.0 38.3 %fusion.24 = f32[2,768,2048]{2,1,0:T(8,128)} fusion(f32[2,768,2048]{2,1,0:T(8,128)S(1)} %multiply_add_fusion.3, f32[2,768,768]{2,1,0:T(8,128)S(1)} %fusion.158, f32[2,768,768]{2,1,0:T(8,128)S(1)} %fusion.157), kind=kOutput, calls=%fused_computation.34 | convolution fusion | flops 28994568192 | bytes 34603008 | tf_op jit(solution)/shard_map/nij,njk->nik/dot_general | solution.py:242
  2065.3 34.7 %fusion.21 = f32[2,768,768]{2,1,0:T(8,128)S(1)} fusion(f32[2,768,2048]{2,1,0:T(8,128)} %fusion.24, f32[2,768,2048]{2,1,0:T(8,128)S(1)} %multiply_add_fusion.3), kind=kOutput, calls=%fused_computation.31 | convolution fusion | flops 28997320704 | bytes 29884416 | tf_op jit(solution)/shard_map/nik,njk->nij/dot_general | solution.py:238
  2102.3 13.2 fusion.159
  2115.5 45.5 %multiply_add_fusion.1 = f32[2,768,2048]{2,1,0:T(8,128)} fusion(f32[2,768,2048]{2,1,0:T(8,128)} %fusion.24, f32[2,768,2048]{2,1,0:T(8,128)} %copy-done.7, f32[2,768,768]{2,1,0:T(8,128)} %fusion.159, f32[2,768,768]{2,1,0:T(8,128)} %copy-done.3), kind=kOutput, calls=%fused_computation.4 | convolution fusion | flops 29013442560 | bytes 47185920 | tf_op jit(solution)/shard_map/nij,njk->nik/dot_general | solution.py:242
  2161.0 35.1 %fusion.160 = f32[2,768,768]{2,1,0:T(8,128)S(1)} fusion(f32[2,768,2048]{2,1,0:T(8,128)} %multiply_add_fusion.1), kind=kOutput, calls=%fused_computation.274 | convolution fusion | flops 28991029248 | bytes 17301504 | tf_op jit(solution)/shard_map/nik,njk->nij/dot_general | solution.py:238
  2196.1 12.0 fusion.161
  2208.2 38.2 %fusion.13 = f32[2,768,2048]{2,1,0:T(8,128)} fusion(f32[2,768,2048]{2,1,0:T(8,128)S(1)} %copy-done.6, f32[2,768,768]{2,1,0:T(8,128)S(1)} %fusion.161, f32[2,768,768]{2,1,0:T(8,128)S(1)} %fusion.160), kind=kOutput, calls=%fused_computation.25 | convolution fusion | flops 28994568192 | bytes 34603008 | tf_op jit(solution)/shard_map/nij,njk->nik/dot_general | solution.py:242
  2246.4 34.6 %fusion.10 = f32[2,768,768]{2,1,0:T(8,128)S(1)} fusion(f32[2,768,2048]{2,1,0:T(8,128)} %fusion.13, f32[2,768,2048]{2,1,0:T(8,128)S(1)} %copy-done.6), kind=kOutput, calls=%fused_computation.22 | convolution fusion | flops 28997320704 | bytes 29884416 | tf_op jit(solution)/shard_map/nik,njk->nij/dot_general | solution.py:238
  2283.1 13.3 fusion.162
  2296.3 45.2 %add_convert_fusion = bf16[2,768,2048]{2,1,0:T(8,128)(2,1)} fusion(f32[2,768,2048]{2,1,0:T(8,128)} %fusion.13, f32[2,768,2048]{2,1,0:T(8,128)} %multiply_add_fusion.1, f32[2,768,768]{2,1,0:T(8,128)} %fusion.162, f32[2,768,768]{2,1,0:T(8,128)} %copy-done.4), kind=kOutput, calls=%fused_computation.2 | convolution fusion | flops 29016588288 | bytes 40894464 | tf_op jit(solution)/shard_map/nij,njk->nik/dot_general | solution.py:242
  2341.6 6.5 copy.181
  2372.6 118.1 %all-to-all-done.1 = bf16[2,8,96,2048]{3,2,0,1:T(8,128)(2,1)} async-done(((bf16[2,8,96,2048]{3,2,0,1:T(8,128)(2,1)}), bf16[2,8,96,2048]{3,2,0,1:T(8,128)(2,1)}, u32[]{:S(2)}, u32[]{:S(2)}) %all-to-all-start.1) | async-done | bytes 6291488 | tf_op jit(solution)/shard_map/all_to_all | solution.py:324
  2490.7 6.5 copy.182
  (257 shorter events, 184.1 us)
Async XLA Ops:
  7.2 13.5 copy-start
  7.2 4.8 copy-start.35
  7.2 115.1 %all-gather.6.cloned.1.call-start = ((), (), s32[]{:S(2)}) async-start(), calls=%async_computation.6 | async-start | bytes 7962624 | tf_op jit(solution)/shard_map/all_gather | solution.py:268
  9.9 178.6 %all-gather.8.cloned.1.call-start = ((), (), s32[]{:S(2)}) async-start(), calls=%async_computation.7 | async-start | bytes 3981312 | tf_op jit(solution)/shard_map/all_gather | solution.py:269
  12.0 5.4 copy-start.50
  12.0 218.9 %all-gather.10.cloned.1.call-start = ((), (), s32[]{:S(2)}) async-start(), calls=%async_computation.8 | async-start | bytes 1327104 | tf_op jit(solution)/shard_map/all_gather | solution.py:270
  12.8 7.9 copy-start.53
  12.8 318.5 %all-gather.12.cloned.1.call-start = ((), (), s32[]{:S(2)}) async-start(), calls=%async_computation.9 | async-start | bytes 7077888 | tf_op jit(solution)/shard_map/all_gather | solution.py:271
  15.2 377.3 %all-gather.14.cloned.1.call-start = ((), (), s32[]{:S(2)}) async-start(), calls=%async_computation.10 | async-start | bytes 3538944 | tf_op jit(solution)/shard_map/all_gather | solution.py:272
  17.2 809.1 %all-reduce.15.cloned.1.call-start = ((), (), s32[]{:S(2)}) async-start(), calls=%async_computation.15 | async-start | bytes 25165824
  19.1 477.4 %copy-start.46 = (f32[2,256]{1,0:T(2,128)}, f32[2,256]{1,0:T(2,128)S(1)}, u32[]{:S(2)}) copy-start(f32[2,256]{1,0:T(2,128)S(1)} %broadcast_multiply_fusion.7) | copy-start | bytes 6148
  20.6 475.9 %copy-start.48 = (f32[2,256]{1,0:T(2,128)}, f32[2,256]{1,0:T(2,128)S(1)}, u32[]{:S(2)}) copy-start(f32[2,256]{1,0:T(2,128)S(1)} %add_rsqrt_fusion.1) | copy-start | bytes 6148
  22.5 166.0 %copy-start.8 = (bf16[2,256,768]{2,1,0:T(8,128)(2,1)S(1)}, bf16[2,256,768]{2,1,0:T(8,128)(2,1)}, u32[]{:S(2)}) copy-start(bf16[2,256,768]{2,1,0:T(8,128)(2,1)} %param.15) | copy-start | bytes 2359300
  126.4 370.1 %copy-start.44 = (f32[2,768]{1,0:T(2,128)}, f32[2,768]{1,0:T(2,128)S(1)}, u32[]{:S(2)}) copy-start(f32[2,768]{1,0:T(2,128)S(1)} %get-tuple-element.164) | copy-start | bytes 18436
  206.6 6.4 copy-start.40
  234.4 195.6 %copy-start.19 = (f32[2,256,768]{2,1,0:T(8,128)}, f32[2,256,768]{2,1,0:T(8,128)S(1)}, u32[]{:S(2)}) copy-start(f32[2,256,768]{2,1,0:T(8,128)S(1)} %get-tuple-element.109) | copy-start | bytes 4718596
  429.9 528.7 %reduce-scatter.15.cloned.1.call-start = ((), (), s32[]{:S(2)}) async-start(), calls=%async_computation.13 | async-start | bytes 7962624
  430.0 8.2 copy-start.34
  430.0 8.2 copy-start.54
  430.0 8.2 copy-start.55
  430.0 8.2 copy-start.57
  438.2 5.0 copy-start.38
  443.3 9.0 copy-start.15
  496.4 694.2 %reduce-scatter.13.cloned.1.call-start = ((), (), s32[]{:S(2)}) async-start(), calls=%async_computation.12 | async-start | bytes 15925248
  543.4 718.8 %reduce-scatter.11.cloned.1.call-start = ((), (), s32[]{:S(2)}) async-start(), calls=%async_computation.11 | async-start | bytes 2654208 | tf_op jit(solution)/shard_map/reduce_scatter | solution.py:303
  547.2 835.3 %reduce-scatter.17.cloned.1.call-start = ((), (), s32[]{:S(2)}) async-start(), calls=%async_computation.14 | async-start | bytes 7077888
  553.6 950.2 %all-reduce.17.cloned.1.call-start = ((), (), s32[]{:S(2)}) async-start(), calls=%async_computation.16 | async-start | bytes 12386304 | tf_op jit(solution)/shard_map/psum | solution.py:307
  1383.7 120.0 %copy-start.43 = (f32[96,768]{1,0:T(8,128)S(1)}, f32[96,768]{1,0:T(8,128)}, u32[]{:S(2)}) copy-start(f32[96,768]{1,0:T(8,128)} %param.27) | copy-start | bytes 884740
  1511.1 4.5 copy-start.25
  1511.2 4.4 copy-start.42
  1521.3 4.4 copy-start.32
  1523.5 4.4 copy-start.31
  1534.5 8.8 copy-start.23
  1873.0 4.5 copy-start.2
  1983.7 81.6 %copy-start.7 = (f32[2,768,2048]{2,1,0:T(8,128)}, f32[2,768,2048]{2,1,0:T(8,128)S(1)}, u32[]{:S(2)}) copy-start(f32[2,768,2048]{2,1,0:T(8,128)S(1)} %multiply_add_fusion.3) | copy-start | bytes 37748740
  2196.1 12.1 copy-start.6
  2348.1 5.4 copy-start.52
  2348.1 5.4 copy-start.51
  2348.1 5.4 copy-start.9
  2348.1 5.5 copy-start.17
  2348.1 5.5 copy-start.45
  2348.1 5.5 copy-start.47
  2348.1 5.5 copy-start.49
  2348.1 142.6 %all-to-all-start.1 = ((bf16[2,8,96,2048]{3,2,0,1:T(8,128)(2,1)}), bf16[2,8,96,2048]{3,2,0,1:T(8,128)(2,1)}, u32[]{:S(2)}, u32[]{:S(2)}) async-start(bf16[2,8,96,2048]{3,2,0,1:T(8,128)(2,1)} %copy.181), calls=%async_computation.2 | async-start | bytes 12582912 | tf_op jit(solution)/shard_map/all_to_all | solution.py:324
  2356.7 6.2 copy-start.11
  2364.7 6.2 copy-start.12
  2497.3 5.1 copy-start.24
  2504.4 4.5 copy-start.1
  (24 other events, 55.8 us)
Sparse Core Ops, SparseCore 0:
  10.8 111.4 all-gather.5
  125.1 63.3 all-gather.7
  191.3 39.5 all-gather.9
  233.5 97.7 all-gather.11
  333.9 58.6 all-gather.13
  430.0 396.2 all-reduce.14
  830.5 128.1 reduce-scatter.14
  962.3 228.2 reduce-scatter.12
  1194.1 68.0 reduce-scatter.10
  1265.6 116.9 reduce-scatter.16
  1385.9 117.8 all-reduce.16
where the time goes:
time: 2530 us; the launch traced here: 2520 us
  waiting for transfers between devices  1380 us (55%)
  matrix products  539 us (21%)
  blocking collectives  279 us (11%)
  local copies, waits for them, and re-layouts  237 us (9%)
  other arithmetic  62.2 us (2%)
    unnamed x15, waiting for transfers between devices  750 us
    all_to_all x1, blocking collectives, local(): lax.all_to_all(outgoing, 'fsdp', split_axis=1, concat_axis=1, tiled=True)  279 us
    dot_general x5, matrix products, orthogonalize(): jnp.einsum('nij,njk->nik', poly, current, precision=HIGHEST)  202 us
    dot_general x5, matrix products, orthogonalize(): gram = jnp.einsum('nik,njk->nij', current, current, precision=HIGHEST)  170 us
    all_to_all x1, waiting for transfers between devices, local(): lax.all_to_all(whole.reshape(items_here, devices, rows_local, FF).astype(...  118 us
    psum x1, waiting for transfers between devices, local(): lax.psum((shards[0], shards[1], shards[2], shards[3], shards[4]), 'dp')  117 us
    all_gather x1, waiting for transfers between devices, local(): lax.all_gather(modulation_master.astype(jnp.bfloat16), 'fsdp', axis=1, ti...  99.9 us
    unnamed x145, local copies, waits for them, and re-layouts  96.9 us
  transfers between devices with their start and end apart: 12, of which 12 were waited for; matrix products, arithmetic and copies ran while one was open for 8% of the time, Pallas kernels for 0%

commit v1 on v0

--- a/solution.py
+++ b/solution.py
@@ -16,6 +16,27 @@
 MOMENTUM_DECAY = 0.9
 LEARN_RATE = 1.0
 HIGHEST = lax.Precision.HIGHEST
+
+
+def joined_along(blocks, dim):
+    blocks = jnp.moveaxis(blocks, 0, dim)
+    shape = blocks.shape
+    return blocks.reshape(*shape[:dim], shape[dim] * shape[dim + 1], *shape[dim + 2 :])
+
+
+def doubled(shard, axis):
+    size, index = (lax.axis_size(axis), lax.axis_index(axis))
+    blocks, bit = (shard[None], 1)
+    while bit < size:
+        other = lax.ppermute(blocks, axis, [(i, i ^ bit) for i in range(size)])
+        low = index & bit == 0
+        blocks = jnp.concatenate([jnp.where(low, blocks, other), jnp.where(low, other, blocks)])
+        bit *= 2
+    return blocks
+
+
+def doubled_up(x, axis, dim):
+    return joined_along(doubled(x, axis), dim)
 
 
 def swish_value(values):
@@ -265,7 +286,7 @@
     masters = (modulation_master, projection_master, output_master, expand_master, shrink_master)
     moments = (modulation_moment, projection_moment, output_moment, expand_moment, shrink_moment)
     gathered = (
-        lax.all_gather(modulation_master.astype(jnp.bfloat16), "fsdp", axis=1, tiled=True),
+        doubled_up(modulation_master.astype(jnp.bfloat16), "fsdp", 1),
         lax.all_gather(projection_master.astype(jnp.bfloat16), "fsdp", axis=1, tiled=True),
         lax.all_gather(output_master.astype(jnp.bfloat16), "fsdp", axis=0, tiled=True),
         lax.all_gather(expand_master.astype(jnp.bfloat16), "fsdp", axis=1, tiled=True),

time: 2530 us -> 2610 us (1.032)
  waiting for transfers between devices: 1380 us -> 1670 us
  blocking collectives: 279 us -> 0 us
    all_to_all x1 -> x0, blocking collectives: 279 us -> none  [local(): lax.all_to_all(outgoing, 'fsdp', split_axis=1, concat_axis=1, tiled=True)]
    ppermute x0 -> x3, waiting for transfers between devices: none -> 236 us  [doubled(): other = lax.ppermute(blocks, axis, [(i, i ^ bit) for i in range(size)])]
    all_to_all x0 -> x1, waiting for transfers between devices: none -> 100 us  [local(): lax.all_to_all(outgoing, 'fsdp', split_axis=1, concat_axis=1, tiled=True)]
    all_to_all x1, waiting for transfers between devices: 118 us -> 74 us  [local(): lax.all_to_all(whole.reshape(items_here, devices, rows_local, FF).astype(...]
    unnamed x145 -> x185, local copies, waits for them, and re-layouts: 96.9 us -> 98.9 us
  transfers between devices with their start and end apart: 12 -> 16, of which waited for: 12 -> 15; matrix products, arithmetic and copies ran while one was open for 8% -> 28% of each run, Pallas kernels for 0% -> 0%
where the time goes in v1:
time: 2610 us; the launch traced here: 2590 us
  waiting for transfers between devices  1670 us (64%)
  matrix products  551 us (21%)
  local copies, waits for them, and re-layouts  254 us (10%)
  other arithmetic  88.3 us (3%)
    unnamed x15, waiting for transfers between devices  747 us
    ppermute x3, waiting for transfers between devices, doubled(): other = lax.ppermute(blocks, axis, [(i, i ^ bit) for i in range(size)])  236 us
    dot_general x5, matrix products, orthogonalize(): jnp.einsum('nij,njk->nik', poly, current, precision=HIGHEST)  203 us
    dot_general x5, matrix products, orthogonalize(): gram = jnp.einsum('nik,njk->nij', current, current, precision=HIGHEST)  170 us
    psum x1, waiting for transfers between devices, local(): lax.psum((shards[0], shards[1], shards[2], shards[3], shards[4]), 'dp')  116 us
    all_to_all x1, waiting for transfers between devices, local(): lax.all_to_all(outgoing, 'fsdp', split_axis=1, concat_axis=1, tiled=True)  100 us
    all_gather x1, waiting for transfers between devices, local(): lax.all_gather(modulation_master.astype(jnp.bfloat16), 'fsdp', axis=1, ti...  99.8 us
    unnamed x185, local copies, waits for them, and re-layouts  98.9 us
  transfers between devices with their start and end apart: 16, of which 15 were waited for; matrix products, arithmetic and copies ran while one was open for 28% of the time, Pallas kernels for 0%

profile of v1, /device:TPU:0, one launch (start us, length us, event | category | flops | bytes accessed | tf_op | source)
XLA Modules:
  0.0 2593.3 jit_solution(9173248239631736890)
XLA Ops:
  22.5 99.8 %all-gather.14.cloned.1.call-done = bf16[6,768,768]{2,1,0:T(8,128)(2,1)} async-done(((bf16[6,96,768]{2,1,0:T(8,128)(2,1)}), bf16[6,768,768]{2,1,0:T(8,128)(2,1)}) %all-gather.14.cloned.1.call-update) | async-done | bytes 7077904 | tf_op jit(solution)/shard_map/all_gather | solution.py:308
  126.4 62.1 %all-gather.6.cloned.1.call-done = bf16[3,768,768]{2,1,0:T(8,128)(2,1)} async-done(((bf16[3,96,768]{2,1,0:T(8,128)(2,1)}), bf16[3,768,768]{2,1,0:T(8,128)(2,1)}) %all-gather.6.cloned.1.call-update) | async-done | bytes 3538960 | tf_op jit(solution)/shard_map/all_gather | solution.py:290
  217.6 13.3 all-gather.8.cloned.1.call-done
  234.7 96.6 %all-gather.10.cloned.1.call-done = bf16[2,768,2048]{2,1,0:T(8,128)(2,1)} async-done(((bf16[2,96,2048]{2,1,0:T(8,128)(2,1)}), bf16[2,768,2048]{2,1,0:T(8,128)(2,1)}) %all-gather.10.cloned.1.call-update) | async-done | bytes 6291472 | tf_op jit(solution)/shard_map/all_gather | solution.py:292
  331.3 8.9 fusion.41
  340.2 52.4 %all-gather.12.cloned.1.call-done = bf16[2048,768]{0,1:T(8,128)(2,1)} async-done(((bf16[2048,96]{0,1:T(8,128)(2,1)}), bf16[2048,768]{0,1:T(8,128)(2,1)}) %all-gather.12.cloned.1.call-update) | async-done | bytes 3145744 | tf_op jit(solution)/shard_map/all_gather | solution.py:293
  392.6 9.3 fusion.84
  403.8 6.8 convolution_bitcast_fusion.1
  410.6 19.4 copy.198
  430.6 8.7 fusion.113
  470.5 6.9 convolution_bitcast_fusion.3
  477.3 10.9 copy.246
  488.2 8.2 copy.252
  496.6 6.9 fusion.100
  505.4 7.0 convolution_bitcast_fusion
  512.4 17.6 copy.244
  530.0 16.3 copy.251
  558.8 267.6 %all-reduce.15.cloned.1.call-done = f32[2,768,2048]{2,0,1:T(2,128)} async-done(((f32[2,768,2048]{2,0,1:T(2,128)}), f32[2,768,2048]{2,0,1:T(2,128)}) %all-reduce.15.cloned.1.call-update) | async-done | bytes 12582928
  829.1 129.6 %reduce-scatter.15.cloned.1.call-done = f32[96,2304]{1,0:T(8,128)} async-done(((f32[768,2304]{1,0:T(8,128)}), f32[96,2304]{1,0:T(8,128)}) %reduce-scatter.15.cloned.1.call-update) | async-done | bytes 884752
  961.8 228.9 %reduce-scatter.13.cloned.1.call-done = f32[96,4608]{1,0:T(8,128)} async-done(((f32[768,4608]{1,0:T(8,128)}), f32[96,4608]{1,0:T(8,128)}) %reduce-scatter.13.cloned.1.call-update) | async-done | bytes 1769488
  1194.4 67.8 %reduce-scatter.11.cloned.1.call-done = f32[96,768]{1,0:T(8,128)} async-done(((f32[768,768]{1,0:T(8,128)}), f32[96,768]{1,0:T(8,128)}) %reduce-scatter.11.cloned.1.call-update) | async-done | bytes 294928 | tf_op jit(solution)/shard_map/reduce_scatter | solution.py:324
  1262.2 120.4 %reduce-scatter.17.cloned.1.call-done = f32[96,2048]{1,0:T(8,128)} async-done(((f32[768,2048]{1,0:T(8,128)}), f32[96,2048]{1,0:T(8,128)}) %reduce-scatter.17.cloned.1.call-update) | async-done | bytes 786448
  1387.5 116.3 %all-reduce.17.cloned.1.call-done = (f32[6,96,768]{1,2,0:T(8,128)}, f32[3,96,768]{1,2,0:T(8,128)}, f32[96,768]{1,0:T(8,128)}, f32[2,96,2048]{2,0,1:T(2,128)}, f32[2048,96]{0,1:T(8,128)}) async-done(((f32[6,96,768]{1,2,0:T(8,128)}, f32[3,96,768]{1,2,0:T(8,128)}, f32[96,768]{1,0:T(8,128)}, f32[2,96,2048]{2,0,1:T(2,128)}, f32[2048,96]{0,1:T(8,128)}), (f32[6,96,768]{1,2,0:T(8,128)}, f32[3,96,768]{1,2,0:T(8,128)}, ...) | async-done | bytes 5308432 | tf_op jit(solution)/shard_map/psum | solution.py:328
  1543.2 34.2 %stack.120 = f32[16,96,2048]{2,0,1:T(8,128)} concatenate(f32[1,96,2048]{2,0,1:T(1,128)} %copy.205, f32[1,96,2048]{2,0,1:T(1,128)} %copy.206, f32[1,96,2048]{2,0,1:T(1,128)} %copy.207, f32[1,96,2048]{2,0,1:T(1,128)} %copy.208, f32[1,96,2048]{2,0,1:T(1,128)} %copy.209, f32[1,96,2048]{2,0,1:T(1,128)} %copy.210, f32[1,96,2048]{2,0,1:T(1,128)} %copy.211, f32[1,96,2048]{2,0,1:T(1,128)} %copy.212, ...), dimensions={0} | concatenate | bytes 25165824 | tf_op jit(solution)/shard_map/stack | solution.py:341
  1577.5 16.4 copy.215
  1601.7 119.3 %collective-permute-done = bf16[1,6,96,768]{3,2,1,0:T(8,128)(2,1)} collective-permute-done((bf16[1,6,96,768]{3,2,1,0:T(8,128)(2,1)S(1)}, bf16[1,6,96,768]{3,2,1,0:T(8,128)(2,1)}, u32[]{:S(2)}, u32[]{:S(2)}) %collective-permute-start) | collective-permute-done | bytes 884768 | tf_op jit(solution)/shard_map/ppermute | solution.py:31
  1723.8 116.9 %collective-permute-done.1 = bf16[2,6,96,768]{3,2,1,0:T(8,128)(2,1)} collective-permute-done((bf16[2,6,96,768]{3,2,1,0:T(8,128)(2,1)S(1)}, bf16[2,6,96,768]{3,2,1,0:T(8,128)(2,1)}, u32[]{:S(2)}, u32[]{:S(2)}) %collective-permute-start.1) | collective-permute-done | bytes 1769504 | tf_op jit(solution)/shard_map/ppermute | solution.py:31
  1849.4 100.5 %all-to-all-done = f32[2,8,96,2048]{3,2,0,1:T(8,128)} async-done(((f32[2,8,96,2048]{3,2,0,1:T(8,128)}), f32[2,8,96,2048]{3,2,0,1:T(8,128)}, u32[]{:S(2)}, u32[]{:S(2)}) %all-to-all-start) | async-done | bytes 12582944 | tf_op jit(solution)/shard_map/all_to_all | solution.py:342
  1956.1 11.3 copy.216
  1967.5 11.9 bitcast_divide_fusion
  1979.4 34.7 %fusion.218 = f32[2,768,768]{2,1,0:T(8,128)S(1)} fusion(f32[2,768,2048]{2,1,0:T(8,128)} %bitcast_divide_fusion), kind=kOutput, calls=%fused_computation.348 | convolution fusion | flops 28991029248 | bytes 17301504 | tf_op jit(solution)/shard_map/nik,njk->nij/dot_general | solution.py:259
  2014.0 13.5 fusion.219
  2027.5 35.0 %multiply_add_fusion.3 = f32[2,768,2048]{2,1,0:T(8,128)S(1)} fusion(f32[2,768,2048]{2,1,0:T(8,128)} %bitcast_divide_fusion, f32[2,768,768]{2,1,0:T(8,128)} %fusion.219, f32[2,768,768]{2,1,0:T(8,128)S(1)} %fusion.218), kind=kOutput, calls=%fused_computation.7 | convolution fusion | flops 29000859648 | bytes 34603008 | tf_op jit(solution)/shard_map/nij,njk->nik/dot_general | solution.py:263
  2062.6 31.2 %fusion.220 = f32[2,768,768]{2,1,0:T(8,128)S(1)} fusion(f32[2,768,2048]{2,1,0:T(8,128)S(1)} %multiply_add_fusion.3), kind=kOutput, calls=%fused_computation.350 | convolution fusion | flops 28991029248 | bytes 17301504 | tf_op jit(solution)/shard_map/nik,njk->nij/dot_general | solution.py:259
  2093.8 12.0 fusion.221
  2105.9 38.3 %fusion.28 = f32[2,768,2048]{2,1,0:T(8,128)} fusion(f32[2,768,2048]{2,1,0:T(8,128)S(1)} %multiply_add_fusion.3, f32[2,768,768]{2,1,0:T(8,128)S(1)} %fusion.221, f32[2,768,768]{2,1,0:T(8,128)S(1)} %fusion.220), kind=kOutput, calls=%fused_computation.42 | convolution fusion | flops 28994568192 | bytes 34603008 | tf_op jit(solution)/shard_map/nij,njk->nik/dot_general | solution.py:263
  2144.2 34.6 %fusion.25 = f32[2,768,768]{2,1,0:T(8,128)S(1)} fusion(f32[2,768,2048]{2,1,0:T(8,128)} %fusion.28, f32[2,768,2048]{2,1,0:T(8,128)S(1)} %multiply_add_fusion.3), kind=kOutput, calls=%fused_computation.39 | convolution fusion | flops 28997320704 | bytes 29884416 | tf_op jit(solution)/shard_map/nik,njk->nij/dot_general | solution.py:259
  2181.0 13.5 fusion.222
  2194.5 45.5 %multiply_add_fusion.1 = f32[2,768,2048]{2,1,0:T(8,128)} fusion(f32[2,768,2048]{2,1,0:T(8,128)} %fusion.28, f32[2,768,2048]{2,1,0:T(8,128)} %copy-done.15, f32[2,768,768]{2,1,0:T(8,128)} %fusion.222, f32[2,768,768]{2,1,0:T(8,128)} %copy-done.4), kind=kOutput, calls=%fused_computation.5 | convolution fusion | flops 29013442560 | bytes 47185920 | tf_op jit(solution)/shard_map/nij,njk->nik/dot_general | solution.py:263
  2239.9 34.8 %fusion.223 = f32[2,768,768]{2,1,0:T(8,128)S(1)} fusion(f32[2,768,2048]{2,1,0:T(8,128)} %multiply_add_fusion.1), kind=kOutput, calls=%fused_computation.353 | convolution fusion | flops 28991029248 | bytes 17301504 | tf_op jit(solution)/shard_map/nik,njk->nij/dot_general | solution.py:259
  2274.8 12.0 fusion.224
  2286.8 38.5 %fusion.17 = f32[2,768,2048]{2,1,0:T(8,128)} fusion(f32[2,768,2048]{2,1,0:T(8,128)S(1)} %copy-done.14, f32[2,768,768]{2,1,0:T(8,128)S(1)} %fusion.224, f32[2,768,768]{2,1,0:T(8,128)S(1)} %fusion.223), kind=kOutput, calls=%fused_computation.33 | convolution fusion | flops 28994568192 | bytes 34603008 | tf_op jit(solution)/shard_map/nij,njk->nik/dot_general | solution.py:263
  2325.4 34.5 %fusion.14 = f32[2,768,768]{2,1,0:T(8,128)S(1)} fusion(f32[2,768,2048]{2,1,0:T(8,128)} %fusion.17, f32[2,768,2048]{2,1,0:T(8,128)S(1)} %copy-done.14), kind=kOutput, calls=%fused_computation.30 | convolution fusion | flops 28997320704 | bytes 29884416 | tf_op jit(solution)/shard_map/nik,njk->nij/dot_general | solution.py:259
  2362.0 13.3 fusion.225
  2375.2 45.2 %add_convert_fusion = bf16[2,768,2048]{2,1,0:T(8,128)(2,1)} fusion(f32[2,768,2048]{2,1,0:T(8,128)} %fusion.17, f32[2,768,2048]{2,1,0:T(8,128)} %multiply_add_fusion.1, f32[2,768,768]{2,1,0:T(8,128)} %fusion.225, f32[2,768,768]{2,1,0:T(8,128)} %copy-done.5), kind=kOutput, calls=%fused_computation.3 | convolution fusion | flops 29016588288 | bytes 40894464 | tf_op jit(solution)/shard_map/nij,njk->nik/dot_general | solution.py:263
  2420.5 6.5 copy.217
  2493.7 74.0 %all-to-all-done.1 = bf16[2,8,96,2048]{3,2,0,1:T(8,128)(2,1)} async-done(((bf16[2,8,96,2048]{3,2,0,1:T(8,128)(2,1)}), bf16[2,8,96,2048]{3,2,0,1:T(8,128)(2,1)}, u32[]{:S(2)}, u32[]{:S(2)}) %all-to-all-start.1) | async-done | bytes 6291488 | tf_op jit(solution)/shard_map/all_to_all | solution.py:345
  2567.7 6.6 copy.218
  (332 shorter events, 261.6 us)
Async XLA Ops:
  7.2 13.5 copy-start
  7.2 4.8 copy-start.44
  7.2 115.1 %all-gather.14.cloned.1.call-start = ((), (), s32[]{:S(2)}) async-start(), calls=%async_computation.10 | async-start | bytes 7962624 | tf_op jit(solution)/shard_map/all_gather | solution.py:308
  9.9 178.6 %all-gather.6.cloned.1.call-start = ((), (), s32[]{:S(2)}) async-start(), calls=%async_computation.6 | async-start | bytes 3981312 | tf_op jit(solution)/shard_map/all_gather | solution.py:290
  12.0 218.8 %all-gather.8.cloned.1.call-start = ((), (), s32[]{:S(2)}) async-start(), calls=%async_computation.7 | async-start | bytes 1327104 | tf_op jit(solution)/shard_map/all_gather | solution.py:291
  12.8 4.6 copy-start.65
  12.8 318.5 %all-gather.10.cloned.1.call-start = ((), (), s32[]{:S(2)}) async-start(), calls=%async_computation.8 | async-start | bytes 7077888 | tf_op jit(solution)/shard_map/all_gather | solution.py:292
  15.2 5.5 copy-start.70
  15.2 377.3 %all-gather.12.cloned.1.call-start = ((), (), s32[]{:S(2)}) async-start(), calls=%async_computation.9 | async-start | bytes 3538944 | tf_op jit(solution)/shard_map/all_gather | solution.py:293
  17.2 809.2 %all-reduce.15.cloned.1.call-start = ((), (), s32[]{:S(2)}) async-start(), calls=%async_computation.15 | async-start | bytes 25165824
  19.1 477.5 %copy-start.61 = (f32[2,256]{1,0:T(2,128)}, f32[2,256]{1,0:T(2,128)S(1)}, u32[]{:S(2)}) copy-start(f32[2,256]{1,0:T(2,128)S(1)} %broadcast_multiply_fusion.8) | copy-start | bytes 6148
  20.6 475.9 %copy-start.63 = (f32[2,256]{1,0:T(2,128)}, f32[2,256]{1,0:T(2,128)S(1)}, u32[]{:S(2)}) copy-start(f32[2,256]{1,0:T(2,128)S(1)} %add_rsqrt_fusion.2) | copy-start | bytes 6148
  20.7 185.9 %copy-start.68 = (pred[2,256]{1,0:T(4,128)(4,1)}, pred[2,256]{1,0:T(4,128)(4,1)S(1)}, u32[]{:S(2)}) copy-start(pred[2,256]{1,0:T(4,128)(4,1)S(1)} %get-tuple-element.189) | copy-start | bytes 1540
  21.8 483.6 %copy-start.57 = (bf16[2,768,1]{1,0,2:T(2,128)(2,1)}, bf16[2,768,1]{1,0,2:T(2,128)(2,1)S(1)}, u32[]{:S(2)}) copy-start(bf16[2,768,1]{1,0,2:T(2,128)(2,1)S(1)} %fusion.175) | copy-start | bytes 9220
  22.5 182.2 %copy-start.35 = (f32[2,256,64]{1,2,0:T(8,128)}, f32[2,256,64]{1,2,0:T(8,128)S(1)}, u32[]{:S(2)}) copy-start(f32[2,256,64]{1,2,0:T(8,128)S(1)} %get-tuple-element.169) | copy-start | bytes 393220
  22.5 182.2 %copy-start.37 = (f32[2,256,64]{1,2,0:T(8,128)}, f32[2,256,64]{1,2,0:T(8,128)S(1)}, u32[]{:S(2)}) copy-start(f32[2,256,64]{1,2,0:T(8,128)S(1)} %get-tuple-element.171) | copy-start | bytes 393220
  22.5 166.0 %copy-start.16 = (bf16[2,256,768]{2,1,0:T(8,128)(2,1)S(1)}, bf16[2,256,768]{2,1,0:T(8,128)(2,1)}, u32[]{:S(2)}) copy-start(bf16[2,256,768]{2,1,0:T(8,128)(2,1)} %param.15) | copy-start | bytes 2359300
  126.4 370.1 %copy-start.59 = (f32[2,768]{1,0:T(2,128)}, f32[2,768]{1,0:T(2,128)S(1)}, u32[]{:S(2)}) copy-start(f32[2,768]{1,0:T(2,128)S(1)} %get-tuple-element.176) | copy-start | bytes 18436
  206.6 6.4 copy-start.50
  234.4 196.2 %copy-start.12 = (f32[2,256,768]{2,1,0:T(8,128)}, f32[2,256,768]{2,1,0:T(8,128)S(1)}, u32[]{:S(2)}) copy-start(f32[2,256,768]{2,1,0:T(8,128)S(1)} %get-tuple-element.109) | copy-start | bytes 4718596
  430.0 528.7 %reduce-scatter.15.cloned.1.call-start = ((), (), s32[]{:S(2)}) async-start(), calls=%async_computation.13 | async-start | bytes 7962624
  430.6 8.7 copy-start.24
  430.6 8.7 copy-start.53
  441.6 104.7 %copy-start.9 = (f32[2,256,768]{2,1,0:T(8,128)}, f32[2,256,768]{2,1,0:T(8,128)S(1)}, u32[]{:S(2)}) copy-start(f32[2,256,768]{2,1,0:T(8,128)S(1)} %get-tuple-element.107) | copy-start | bytes 4718596
  496.5 694.2 %reduce-scatter.13.cloned.1.call-start = ((), (), s32[]{:S(2)}) async-start(), calls=%async_computation.12 | async-start | bytes 15925248
  496.5 7.0 copy-start.54
  496.6 7.0 copy-start.72
  496.6 7.0 copy-start.75
  546.3 716.0 %reduce-scatter.11.cloned.1.call-start = ((), (), s32[]{:S(2)}) async-start(), calls=%async_computation.11 | async-start | bytes 2654208 | tf_op jit(solution)/shard_map/reduce_scatter | solution.py:324
  549.7 833.0 %reduce-scatter.17.cloned.1.call-start = ((), (), s32[]{:S(2)}) async-start(), calls=%async_computation.14 | async-start | bytes 7077888
  557.0 946.9 %all-reduce.17.cloned.1.call-start = ((), (), s32[]{:S(2)}) async-start(), calls=%async_computation.16 | async-start | bytes 12386304 | tf_op jit(solution)/shard_map/psum | solution.py:328
  1385.6 118.2 %copy-start.56 = (f32[96,768]{1,0:T(8,128)S(1)}, f32[96,768]{1,0:T(8,128)}, u32[]{:S(2)}) copy-start(f32[96,768]{1,0:T(8,128)} %param.27) | copy-start | bytes 884740
  1511.1 4.4 copy-start.30
  1521.3 4.4 copy-start.41
  1593.9 5.7 copy-start.2
  1593.9 356.0 %all-to-all-start = ((f32[2,8,96,2048]{3,2,0,1:T(8,128)}), f32[2,8,96,2048]{3,2,0,1:T(8,128)}, u32[]{:S(2)}, u32[]{:S(2)}) async-start(f32[2,8,96,2048]{3,2,0,1:T(8,128)} %copy.215), calls=%async_computation.1 | async-start | bytes 25165824 | tf_op jit(solution)/shard_map/all_to_all | solution.py:342
  1599.6 121.4 %collective-permute-start = (bf16[1,6,96,768]{3,2,1,0:T(8,128)(2,1)S(1)}, bf16[1,6,96,768]{3,2,1,0:T(8,128)(2,1)}, u32[]{:S(2)}, u32[]{:S(2)}) collective-permute-start(bf16[1,6,96,768]{3,2,1,0:T(8,128)(2,1)S(1)} %convert_bitcast_fusion), channel_id=1, source_target_pairs={{0,1},{1,0},{2,3},{3,2},{4,5},{5,4},{6,7},{7,6},{8,9},{9,8},{10,11... | collective-permute-start | bytes 2654216 | tf_op jit(solution)/shard_map/ppermute | solution.py:31
  1723.4 117.2 %collective-permute-start.1 = (bf16[2,6,96,768]{3,2,1,0:T(8,128)(2,1)S(1)}, bf16[2,6,96,768]{3,2,1,0:T(8,128)(2,1)}, u32[]{:S(2)}, u32[]{:S(2)}) collective-permute-start(bf16[2,6,96,768]{3,2,1,0:T(8,128)(2,1)S(1)} %pad_maximum_fusion.5), channel_id=1, source_target_pairs={{0,2},{1,3},{2,0},{3,1},{4,6},{5,7},{6,4},{7,5},{8,10},{9,11},{10,... | collective-permute-start | bytes 5308424 | tf_op jit(solution)/shard_map/ppermute | solution.py:31
  1845.5 586.7 %collective-permute-start.2 = (bf16[4,6,96,768]{3,2,1,0:T(8,128)(2,1)}, bf16[4,6,96,768]{3,2,1,0:T(8,128)(2,1)}, u32[]{:S(2)}, u32[]{:S(2)}) collective-permute-start(bf16[4,6,96,768]{3,2,1,0:T(8,128)(2,1)} %pad_maximum_fusion.1), channel_id=1, source_target_pairs={{0,4},{1,5},{2,6},{3,7},{4,0},{5,1},{6,2},{7,3},{8,12},{9,13},{10,... | collective-permute-start | bytes 10616840 | tf_op jit(solution)/shard_map/ppermute | solution.py:31
  2062.6 81.6 %copy-start.15 = (f32[2,768,2048]{2,1,0:T(8,128)}, f32[2,768,2048]{2,1,0:T(8,128)S(1)}, u32[]{:S(2)}) copy-start(f32[2,768,2048]{2,1,0:T(8,128)S(1)} %multiply_add_fusion.3) | copy-start | bytes 37748740
  2274.7 12.1 copy-start.14
  2427.0 5.3 copy-start.7
  2427.0 140.8 %all-to-all-start.1 = ((bf16[2,8,96,2048]{3,2,0,1:T(8,128)(2,1)}), bf16[2,8,96,2048]{3,2,0,1:T(8,128)(2,1)}, u32[]{:S(2)}, u32[]{:S(2)}) async-start(bf16[2,8,96,2048]{3,2,0,1:T(8,128)(2,1)} %copy.217), calls=%async_computation.2 | async-start | bytes 12582912 | tf_op jit(solution)/shard_map/all_to_all | solution.py:345
  2463.0 5.8 slice-start
  2477.6 6.2 copy-start.19
  2485.6 6.2 copy-start.20
  2574.3 4.3 copy-start.45
  2574.3 5.1 copy-start.29
  (48 other events, 112.5 us)
Sparse Core Ops, SparseCore 0:
  10.8 111.4 all-gather.13
  125.1 63.3 all-gather.5
  191.3 39.5 all-gather.7
  233.5 97.7 all-gather.9
  333.9 58.6 all-gather.11
  430.1 396.2 all-reduce.14
  830.5 128.1 reduce-scatter.14
  962.3 228.2 reduce-scatter.12
  1194.1 68.0 reduce-scatter.10
  1265.7 116.9 reduce-scatter.16
  1385.9 117.8 all-reduce.16
